TPU v7x, 128 devices: a whole 4x4x4 slice. The times are simulated.
128 devices in a mesh: sample: 16 (over y, x), col: 8 (over z, core).
Axes of the slice: x: 4, y: 4, z: 4, core: 2. Of those that a mesh axis runs over, the one named last changes fastest.
Arguments:
- block_inputs: bfloat16 [2048, 17, 17, 768], P(('sample', 'col')), may hold values from 0 to 100, as said below
- first_entry: bfloat16 [1, 1, 768, 384], replicated, may hold values from -0.3125 to 0.3125
- first_wide: bfloat16 [3, 3, 192, 320], replicated, may hold values from -0.21875 to 0.21875
- first_row: bfloat16 [1, 7, 192, 192], replicated, may hold values from -0.25 to 0.25
- first_column: bfloat16 [7, 1, 192, 192], replicated, may hold values from -0.25 to 0.25
- first_reduce: bfloat16 [3, 3, 192, 192], replicated, may hold values from -0.21875 to 0.21875
- second_entry: bfloat16 [1, 1, 1280, 1152], replicated, may hold values from -0.25 to 0.25
- second_row: bfloat16 [1, 3, 384, 384], replicated, may hold values from -0.25 to 0.25
- second_column: bfloat16 [3, 1, 384, 384], replicated, may hold values from -0.25 to 0.25
- second_deep: bfloat16 [3, 3, 448, 384], replicated, may hold values from -0.125 to 0.125
- deep_row: bfloat16 [1, 3, 384, 384], replicated, may hold values from -0.25 to 0.25
- deep_column: bfloat16 [3, 1, 384, 384], replicated, may hold values from -0.25 to 0.25
- pool_project: bfloat16 [1, 1, 1280, 192], replicated, may hold values from -0.25 to 0.25
Outputs:
- feature_mean: float32 [2048], replicated
- covariance: float32 [2048, 2048], P('sample', 'col')
Inputs may be any that keep to these rules, and one draw needn't show every extreme that they name: `block_inputs`: nonnegative activations.
All inputs are finite; a program needn't handle non-finite values.
Results may differ from a plain program's by a relative error of at most 0.0003.
Values sent between devices are 32-bit elements; how exact they have to be, the bound alone decides.
No kernel may reach another device: no remote copies, remote signals or barrier semaphores. Data moves between devices by JAX's collectives and lax.ppermute only.
A program may use at most 128 MiB of HBM per device.

v0:
```python
import jax
import jax.numpy as jnp
from jax import lax
from jax.sharding import PartitionSpec as P


def combined_all(part, axis, combine):
    gathered = jax.tree.map(lambda a: lax.all_gather(a, axis), part)

    def take(source):
        return jax.tree.map(lambda a: lax.dynamic_index_in_dim(a, source, 0, False), gathered)

    return lax.fori_loop(
        1, lax.axis_size(axis), lambda source, state: combine(state, take(source)), take(0)
    )


def rectify(inputs, kernel, stride, padding):
    result = lax.conv_general_dilated(
        inputs,
        kernel,
        (stride, stride),
        padding,
        dimension_numbers=("NHWC", "HWIO", "NHWC"),
        preferred_element_type=jnp.float32,
    )
    return jnp.maximum(result, 0.0).astype(jnp.bfloat16)


def spatial_mean(inputs):
    return jnp.mean(inputs.astype(jnp.float32), axis=(1, 2))


def network(
    block_inputs,
    first_entry,
    first_wide,
    first_row,
    first_column,
    first_reduce,
    second_entry,
    second_row,
    second_column,
    second_deep,
    deep_row,
    deep_column,
    pool_project,
):
    no_margin = ((0, 0), (0, 0))
    entry_out = rectify(block_inputs, first_entry, 1, no_margin)
    half_width = first_wide.shape[2]
    wide_out = rectify(entry_out[..., :half_width], first_wide, 2, no_margin)
    tower_out = rectify(entry_out[..., half_width:], first_row, 1, ((0, 0), (3, 3)))
    tower_out = rectify(tower_out, first_column, 1, ((3, 3), (0, 0)))
    tower_out = rectify(tower_out, first_reduce, 2, no_margin)
    maximum = lax.reduce_window(
        block_inputs,
        jnp.array(-jnp.inf, block_inputs.dtype),
        lax.max,
        (1, 3, 3, 1),
        (1, 2, 2, 1),
        "VALID",
    )
    middle = jnp.concatenate([wide_out, tower_out, maximum], axis=3)
    second = rectify(middle, second_entry, 1, no_margin)
    branch_width = second_row.shape[2]
    deep_width = second_deep.shape[2]
    plain_width = second_entry.shape[3] - branch_width - deep_width
    plain_out = second[..., :plain_width]
    branch_in = second[..., plain_width : plain_width + branch_width]
    deep_in = second[..., plain_width + branch_width :]
    row_a = rectify(branch_in, second_row, 1, ((0, 0), (1, 1)))
    col_a = rectify(branch_in, second_column, 1, ((1, 1), (0, 0)))
    deep_out = rectify(deep_in, second_deep, 1, ((1, 1), (1, 1)))
    row_b = rectify(deep_out, deep_row, 1, ((0, 0), (1, 1)))
    col_b = rectify(deep_out, deep_column, 1, ((1, 1), (0, 0)))
    pool_pad = ((0, 0), (1, 1), (1, 1), (0, 0))
    summed = lax.reduce_window(
        middle.astype(jnp.float32),
        jnp.array(0.0, jnp.float32),
        lax.add,
        (1, 3, 3, 1),
        (1, 1, 1, 1),
        pool_pad,
    )
    ones_map = jnp.ones((1, middle.shape[1], middle.shape[2], 1), jnp.float32)
    cell_count = lax.reduce_window(
        ones_map, jnp.array(0.0, jnp.float32), lax.add, (1, 3, 3, 1), (1, 1, 1, 1), pool_pad
    )
    averaged = (summed / cell_count).astype(jnp.bfloat16)
    pooled = rectify(averaged, pool_project, 1, no_margin)
    return jnp.concatenate(
        [
            spatial_mean(plain_out),
            spatial_mean(row_a),
            spatial_mean(col_a),
            spatial_mean(row_b),
            spatial_mean(col_b),
            spatial_mean(pooled),
        ],
        axis=1,
    )


def local(
    block_inputs,
    first_entry,
    first_wide,
    first_row,
    first_column,
    first_reduce,
    second_entry,
    second_row,
    second_column,
    second_deep,
    deep_row,
    deep_column,
    pool_project,
):
    features = network(
        block_inputs,
        first_entry,
        first_wide,
        first_row,
        first_column,
        first_reduce,
        second_entry,
        second_row,
        second_column,
        second_deep,
        deep_row,
        deep_column,
        pool_project,
    )
    gathered = lax.all_gather(features, "col", axis=0, tiled=True)
    width = gathered.shape[1]
    col_width = width // lax.axis_size("col")
    col_start = lax.axis_index("col") * col_width
    row_width = width // lax.axis_size("sample")
    row_start = lax.axis_index("sample") * row_width
    group_images = gathered.shape[0]
    total_images = group_images * lax.axis_size("sample")
    highest = lax.Precision.HIGHEST
    group_mean = jnp.sum(gathered, axis=0) / group_images
    centered = gathered - group_mean
    columns = lax.dynamic_slice_in_dim(centered, col_start, col_width, 1)
    moments = jnp.einsum(
        "nf,nc->fc", centered, columns, precision=highest, preferred_element_type=jnp.float32
    )
    members = jnp.array(group_images, jnp.float32)

    def combine(earlier, latter):
        count_a, mean_a, moment_a = earlier
        count_b, mean_b, moment_b = latter
        count_all = count_a + count_b
        mean_gap = mean_b - mean_a
        gap_columns = lax.dynamic_slice_in_dim(mean_gap, col_start, col_width, 0)
        mean_all = mean_a + mean_gap * (count_b / count_all)
        moment_all = (
            moment_a + moment_b + jnp.outer(mean_gap, gap_columns) * (count_a * count_b / count_all)
        )
        return (count_all, mean_all, moment_all)

    merged_count, feature_mean, merged_moments = combined_all(
        (members, group_mean, moments), "sample", combine
    )
    covariance = lax.dynamic_slice_in_dim(merged_moments, row_start, row_width, 0) / (
        total_images - 1
    )
    return (feature_mean, covariance)


def solution(mesh):
    placed = (
        P(("sample", "col"), None, None, None),
        P(),
        P(),
        P(),
        P(),
        P(),
        P(),
        P(),
        P(),
        P(),
        P(),
        P(),
        P(),
    )
    return jax.shard_map(
        local, mesh=mesh, in_specs=placed, out_specs=(P(), P("sample", "col")), check_vma=False
    )
```

profile of v0, /device:TPU:1, one launch (start us, length us, event | category | flops | bytes accessed | tf_op | source)
XLA Modules:
  0.0 411.1 jit_solution(14171061432312267951)
XLA Ops:
  7.2 5.7 %fusion.26 = bf16[16,8,8,768]{3,0,2,1:T(8,128)(2,1)} fusion(bf16[16,17,17,768]{3,0,2,1:T(8,128)(2,1)} %param.15), kind=kOutput, calls=%fused_computation.51 | output fusion | flops 6291456 | bytes 8675328 | tf_op jit(solution)/shard_map/reduce_window | solution.py:56
  12.9 4.1 maximum_convert_fusion
  17.1 3.0 maximum_convert_fusion.11
  20.1 11.7 %fusion.7 = bf16[16,17,17,192]{3,0,2,1:T(8,128)(2,1)} fusion(bf16[1,7,192,192]{3,2,1,0:T(8,128)(2,1)S(1)} %copy-done.10, bf16[16,17,17,384]{3,0,2,1:T(8,128)(2,1)S(1)} %maximum_convert_fusion), kind=kOutput, calls=%fused_computation.13 | convolution fusion | flops 2145779712 | bytes 4831232 | tf_op jit(solution)/shard_map/conv_general_dilated | solution.py:19
  31.7 9.4 %fusion.14 = bf16[16,8,8,192]{3,0,2,1:T(8,128)(2,1)} fusion(bf16[3,3,192,192]{3,2,1,0:T(8,128)(2,1)} %param.20, bf16[7,1,192,192]{3,2,1,0:T(8,128)(2,1)} %param.19, bf16[16,17,17,192]{3,0,2,1:T(8,128)(2,1)} %fusion.7), kind=kOutput, calls=%fused_computation.31 | convolution fusion | flops 2830089216 | bytes 3348480 | tf_op jit(solution)/shard_map/conv_general_dilated | solution.py:19
  41.1 5.4 %concatenate.6 = bf16[16,8,8,1280]{3,0,2,1:T(8,128)(2,1)} concatenate(bf16[16,8,8,320]{3,0,2,1:T(8,128)(2,1)} %maximum_convert_fusion.11, bf16[16,8,8,192]{3,0,2,1:T(8,128)(2,1)} %fusion.14, bf16[16,8,8,768]{3,0,2,1:T(8,128)(2,1)} %fusion.26), dimensions={3} | concatenate | bytes 5242880 | tf_op jit(solution)/shard_map/concatenate | solution.py:64
  46.5 6.3 %fusion.5 = bf16[16,8,8,1152]{3,0,2,1:T(8,128)(2,1)S(1)} fusion(bf16[16,8,8,1280]{3,0,2,1:T(8,128)(2,1)} %concatenate.6, bf16[1,1,1280,1152]{3,2,1,0:T(8,128)(2,1)} %param.21), kind=kOutput, calls=%fused_computation.11 | convolution fusion | flops 3022258176 | bytes 7929856 | tf_op jit(solution)/shard_map/conv_general_dilated | solution.py:19
  52.9 1.6 multiply_convert_fusion
  54.5 0.9 fusion.17
  55.4 0.2 convert_reduce_fusion.4
  55.5 0.1 copy-done.6
  55.6 1.5 convert_reduce_fusion.2
  57.1 1.5 convert_reduce_fusion.3
  58.7 4.6 %maximum_convert_fusion.8 = bf16[16,8,8,384]{3,0,2,1:T(8,128)(2,1)S(1)} fusion(bf16[3,3,448,384]{3,2,1,0:T(8,128)(2,1)S(1)} %copy-done, bf16[16,8,8,1152]{3,0,2,1:T(8,128)(2,1)S(1)} %fusion.5), kind=kOutput, calls=%fused_computation.22 | convolution fusion | flops 2665218048 | bytes 4931584 | tf_op jit(solution)/shard_map/conv_general_dilated | solution.py:19
  63.3 1.5 convert_reduce_fusion
  64.8 1.7 convert_reduce_fusion.1
  66.6 0.8 concatenate.7
  67.4 27.1 %all-gather.5.cloned.1.call-done = f32[128,2048]{1,0:T(8,128)} async-done(((f32[16,2048]{1,0:T(8,128)}), f32[128,2048]{1,0:T(8,128)}) %all-gather.5.cloned.1.call-update) | async-done | bytes 1048592 | tf_op jit(solution)/shard_map/all_gather | solution.py:135
  94.5 1.3 reduce_sum.69
  95.8 1.3 broadcast_subtract_fusion
  97.2 3.2 fusion.21
  100.4 0.6 dynamic-slice
  101.0 0.8 dynamic-update-slice
  101.7 34.3 %all-reduce = f32[16]{0:T(128)S(1)} all-reduce(f32[16]{0:T(128)S(1)} %dynamic-update-slice), channel_id=1, replica_groups=mesh['sample'=16,'col'=8] {'sample'}, use_global_device_ids=true, to_apply=%add | all-reduce | flops 16 | bytes 128
  136.1 17.7 %all-gather = f32[32768]{0:T(1024)S(1)} all-gather(f32[2048]{0:T(1024)S(1)} %broadcast_multiply_fusion.6), channel_id=2, replica_groups=mesh['sample'=16,'col'=8] {'sample'}, dimensions={0}, use_global_device_ids=true | all-gather | bytes 139264 | tf_op jit(solution)/shard_map/all_gather | solution.py:8
  153.9 143.4 %all-gather.7.cloned.1.call-done = f32[32768,256]{1,0:T(8,128)} async-done(((f32[2048,256]{1,0:T(8,128)}), f32[32768,256]{1,0:T(8,128)}) %all-gather.7.cloned.1.call-update) | async-done | bytes 33554448 | tf_op jit(solution)/shard_map/all_gather | solution.py:8
  297.3 3.0 slice.31
  300.3 102.3 %while.21 = (s32[]{:T(128)}, f32[]{:T(128)}, f32[2048]{0:T(1024)S(1)}, f32[2048,256]{1,0:T(8,128)}, f32[16]{0:T(128)S(1)}, /*index=5*/f32[16,2048]{1,0:T(8,128)S...) while((s32[]{:T(128)}, f32[]{:T(128)}, f32[2048]{0:T(1024)S(1)}, ...), condition=%wide.region_10.11_spmd, body=%wide.region_9.0_spmd.sunk | while | flops 2103305 | bytes 6352095 | solution.py:13
  300.3 0.7 dynamic_slice.82
  303.2 0.1 dynamic_slice.83
  303.2 3.9 fusion.47
  307.2 0.7 dynamic_slice.82
  310.0 0.1 dynamic_slice.83
  310.1 3.9 fusion.47
  314.0 0.7 dynamic_slice.82
  316.8 0.1 dynamic_slice.83
  316.9 3.9 fusion.47
  320.8 0.7 dynamic_slice.82
  323.6 0.1 dynamic_slice.83
  323.7 3.9 fusion.47
  327.6 0.7 dynamic_slice.82
  330.4 0.1 dynamic_slice.83
  330.5 3.9 fusion.47
  334.4 0.7 dynamic_slice.82
  337.4 3.9 fusion.47
  341.3 0.7 dynamic_slice.82
  344.2 3.9 fusion.47
  348.1 0.7 dynamic_slice.82
  351.0 3.9 fusion.47
  354.9 0.7 dynamic_slice.82
  357.8 3.9 fusion.47
  361.7 0.7 dynamic_slice.82
  364.6 3.9 fusion.47
  368.6 0.7 dynamic_slice.82
  371.5 3.9 fusion.47
  375.4 0.7 dynamic_slice.82
  378.3 3.9 fusion.47
  382.2 0.7 dynamic_slice.82
  385.1 3.9 fusion.47
  389.0 0.7 dynamic_slice.82
  391.9 3.9 fusion.47
  395.8 0.7 dynamic_slice.82
  398.7 3.9 fusion.47
  402.7 1.6 dynamic-slice_multiply_fusion
  (79 shorter events, 1.4 us)
Async XLA Ops:
  7.2 51.5 %copy-start = (bf16[3,3,448,384]{3,2,1,0:T(8,128)(2,1)S(1)}, bf16[3,3,448,384]{3,2,1,0:T(8,128)(2,1)}, u32[]{:S(2)}) copy-start(bf16[3,3,448,384]{3,2,1,0:T(8,128)(2,1)} %param.24) | copy-start | bytes 9289732
  7.2 87.4 %all-gather.5.cloned.1.call-start = ((), (), s32[]{:S(2)}) async-start(), calls=%async_computation | async-start | bytes 1179648 | tf_op jit(solution)/shard_map/all_gather | solution.py:135
  7.2 5.7 %copy-start.2 = (bf16[16,17,17,768]{3,0,2,1:T(8,128)(2,1)S(1)}, bf16[16,17,17,768]{3,0,2,1:T(8,128)(2,1)}, u32[]{:S(2)}) copy-start(bf16[16,17,17,768]{3,0,2,1:T(8,128)(2,1)} %param.15) | copy-start | bytes 21307396
  7.2 5.7 %copy-start.11 = (bf16[1,1,768,384]{3,2,1,0:T(8,128)(2,1)S(1)}, bf16[1,1,768,384]{3,2,1,0:T(8,128)(2,1)}, u32[]{:S(2)}) copy-start(bf16[1,1,768,384]{3,2,1,0:T(8,128)(2,1)} %param.16) | copy-start | bytes 1769476
  12.9 4.1 %copy-start.5 = (bf16[3,3,192,320]{3,2,1,0:T(8,128)(2,1)S(1)}, bf16[3,3,192,320]{3,2,1,0:T(8,128)(2,1)}, u32[]{:S(2)}) copy-start(bf16[3,3,192,320]{3,2,1,0:T(8,128)(2,1)} %param.17) | copy-start | bytes 3317764
  17.1 3.0 copy-start.10
  46.5 6.3 %copy-start.1 = (bf16[16,8,8,1280]{3,0,2,1:T(8,128)(2,1)S(1)}, bf16[16,8,8,1280]{3,0,2,1:T(8,128)(2,1)}, u32[]{:S(2)}) copy-start(bf16[16,8,8,1280]{3,0,2,1:T(8,128)(2,1)} %concatenate.6) | copy-start | bytes 7864324
  46.5 6.3 %copy-start.4 = (f32[8,8]{1,0:T(8,128)S(1)}, f32[8,8]{1,0:T(8,128)}, u32[]{:S(2)}) copy-start(f32[8,8]{1,0:T(8,128)} %constant.112.clone.1) | copy-start | bytes 772
  52.9 1.6 copy-start.12
  54.5 1.2 copy-start.6
  55.6 1.5 copy-start.7
  58.7 4.6 %copy-start.8 = (bf16[3,1,384,384]{3,2,1,0:T(8,128)(2,1)S(1)}, bf16[3,1,384,384]{3,2,1,0:T(8,128)(2,1)}, u32[]{:S(2)}) copy-start(bf16[3,1,384,384]{3,2,1,0:T(8,128)(2,1)} %param.26) | copy-start | bytes 2654212
  63.3 1.5 copy-start.9
  67.3 230.0 %all-gather.7.cloned.1.call-start = ((), (), s32[]{:S(2)}) async-start(), calls=%async_computation.1 | async-start | bytes 35651584 | tf_op jit(solution)/shard_map/all_gather | solution.py:8
  97.2 3.2 copy-start.13
  402.7 1.6 copy-start.3
Sparse Core Ops, SparseCore 0:
  67.5 27.0 all-gather.4
  100.5 196.7 all-gather.6
where the time goes:
time: 412 us; the launch traced here: 411 us
  waiting for transfers between devices  171 us (42%)
  other arithmetic  70.5 us (17%)
  blocking collectives  52.1 us (13%)
  matrix products  49.3 us (12%)
  loops' own time  32.1 us (8%)
  local copies, waits for them, and re-layouts  22.1 us (5%)
  between operations  14.4 us (3%)
    all_gather x1, waiting for transfers between devices, combined_all(): gathered = jax.tree.map(lambda a: lax.all_gather(a, axis), part)  143 us
    add x15, other arithmetic, combine(): moment_a + moment_b  58.7 us
    conv_general_dilated x11, matrix products, rectify(): lax.conv_general_dilated(inputs, kernel, (stride, stride), padding, dimen...  46.2 us
    unnamed x1, blocking collectives  34.3 us
    another operation x1, loops' own time, combined_all(): lax.fori_loop(1, lax.axis_size(axis), lambda source, state: combine(state...  32.1 us
    all_gather x1, waiting for transfers between devices, local(): gathered = lax.all_gather(features, 'col', axis=0, tiled=True)  27.1 us
    all_gather x1, blocking collectives, combined_all(): gathered = jax.tree.map(lambda a: lax.all_gather(a, axis), part)  17.7 us
    dynamic_slice x32, local copies, waits for them, and re-layouts, take(): lax.dynamic_index_in_dim(a, source, 0, False)  13.2 us
  transfers between devices with their start and end apart: 2, of which 2 were waited for; matrix products, arithmetic and copies ran while one was open for 0% of the time, Pallas kernels for 0%

commit v1 on v0

--- a/solution.py
+++ b/solution.py
@@ -2,6 +2,7 @@
 import jax.numpy as jnp
 from jax import lax
 from jax.sharding import PartitionSpec as P
+from jax.lax import all_to_all, axis_size
 
 
 def combined_all(part, axis, combine):
@@ -132,7 +133,9 @@
         deep_column,
         pool_project,
     )
-    gathered = lax.all_gather(features, "col", axis=0, tiled=True)
+    gathered = jnp.concatenate(
+        all_to_all(jnp.stack([features for _ in range(axis_size("col"))]), "col", 0, 0), axis=0
+    )
     width = gathered.shape[1]
     col_width = width // lax.axis_size("col")
     col_start = lax.axis_index("col") * col_width

time: 412 us -> 407 us (0.988)
  waiting for transfers between devices: 171 us -> 158 us
  starting transfers between devices: 0.08 us -> 6.81 us
    all_gather x1 -> x0, waiting for transfers between devices: 27.1 us -> none  [local(): gathered = lax.all_gather(features, 'col', axis=0, tiled=True)]
    all_to_all x0 -> x1, waiting for transfers between devices: none -> 15.1 us  [local(): all_to_all(jnp.stack([features for _ in range(axis_size('col'))]), 'col',...]
    all_to_all x0 -> x1, starting transfers between devices: none -> 6.81 us  [local(): all_to_all(jnp.stack([features for _ in range(axis_size('col'))]), 'col',...]
where the time goes in v1:
time: 407 us; the launch traced here: 406 us
  waiting for transfers between devices  158 us (39%)
  other arithmetic  70.5 us (17%)
  blocking collectives  52.5 us (13%)
  matrix products  49.3 us (12%)
  loops' own time  32.1 us (8%)
  local copies, waits for them, and re-layouts  22.6 us (6%)
  between operations  14.4 us (4%)
  starting transfers between devices  6.81 us (2%)
    all_gather x1, waiting for transfers between devices, combined_all(): gathered = jax.tree.map(lambda a: lax.all_gather(a, axis), part)  143 us
    add x15, other arithmetic, combine(): moment_a + moment_b  58.7 us
    conv_general_dilated x11, matrix products, rectify(): lax.conv_general_dilated(inputs, kernel, (stride, stride), padding, dimen...  46.1 us
    unnamed x1, blocking collectives  35 us
    another operation x1, loops' own time, combined_all(): lax.fori_loop(1, lax.axis_size(axis), lambda source, state: combine(state...  32.1 us
    all_gather x1, blocking collectives, combined_all(): gathered = jax.tree.map(lambda a: lax.all_gather(a, axis), part)  17.6 us
    all_to_all x1, waiting for transfers between devices, local(): all_to_all(jnp.stack([features for _ in range(axis_size('col'))]), 'col',...  15.1 us
    dynamic_slice x32, local copies, waits for them, and re-layouts, take(): lax.dynamic_index_in_dim(a, source, 0, False)  13.2 us
  transfers between devices with their start and end apart: 2, of which 2 were waited for; matrix products, arithmetic and copies ran while one was open for 0% of the time, Pallas kernels for 0%

profile of v1, /device:TPU:1, one launch (start us, length us, event | category | flops | bytes accessed | tf_op | source)
XLA Modules:
  0.0 406.5 jit_solution(2246159376834056518)
XLA Ops:
  7.2 5.7 %fusion.26 = bf16[16,8,8,768]{3,0,2,1:T(8,128)(2,1)} fusion(bf16[16,17,17,768]{3,0,2,1:T(8,128)(2,1)} %param.15), kind=kOutput, calls=%fused_computation.51 | output fusion | flops 6291456 | bytes 8675328 | tf_op jit(solution)/shard_map/reduce_window | solution.py:57
  12.9 4.1 %maximum_convert_fusion = bf16[16,17,17,384]{3,0,2,1:T(8,128)(2,1)S(1)} fusion(bf16[16,17,17,768]{3,0,2,1:T(8,128)(2,1)S(1)} %copy-done.2, bf16[1,1,768,384]{3,2,1,0:T(8,128)(2,1)S(1)} %copy-done.11), kind=kOutput, calls=%fused_computation.4 | convolution fusion | flops 2730897408 | bytes 11243520 | tf_op jit(solution)/shard_map/conv_general_dilated | solution.py:20
  17.0 3.0 maximum_convert_fusion.11
  20.0 11.7 %fusion.7 = bf16[16,17,17,192]{3,0,2,1:T(8,128)(2,1)} fusion(bf16[1,7,192,192]{3,2,1,0:T(8,128)(2,1)S(1)} %copy-done.10, bf16[16,17,17,384]{3,0,2,1:T(8,128)(2,1)S(1)} %maximum_convert_fusion), kind=kOutput, calls=%fused_computation.13 | convolution fusion | flops 2145779712 | bytes 4831232 | tf_op jit(solution)/shard_map/conv_general_dilated | solution.py:20
  31.7 9.4 %fusion.14 = bf16[16,8,8,192]{3,0,2,1:T(8,128)(2,1)} fusion(bf16[3,3,192,192]{3,2,1,0:T(8,128)(2,1)} %param.20, bf16[7,1,192,192]{3,2,1,0:T(8,128)(2,1)} %param.19, bf16[16,17,17,192]{3,0,2,1:T(8,128)(2,1)} %fusion.7), kind=kOutput, calls=%fused_computation.31 | convolution fusion | flops 2830089216 | bytes 3348480 | tf_op jit(solution)/shard_map/conv_general_dilated | solution.py:20
  41.1 5.4 %concatenate.6 = bf16[16,8,8,1280]{3,0,2,1:T(8,128)(2,1)} concatenate(bf16[16,8,8,320]{3,0,2,1:T(8,128)(2,1)} %maximum_convert_fusion.11, bf16[16,8,8,192]{3,0,2,1:T(8,128)(2,1)} %fusion.14, bf16[16,8,8,768]{3,0,2,1:T(8,128)(2,1)} %fusion.26), dimensions={3} | concatenate | bytes 5242880 | tf_op jit(solution)/shard_map/concatenate | solution.py:65
  46.5 6.3 %fusion.5 = bf16[16,8,8,1152]{3,0,2,1:T(8,128)(2,1)S(1)} fusion(bf16[16,8,8,1280]{3,0,2,1:T(8,128)(2,1)} %concatenate.6, bf16[1,1,1280,1152]{3,2,1,0:T(8,128)(2,1)} %param.21), kind=kOutput, calls=%fused_computation.11 | convolution fusion | flops 3022258176 | bytes 7929856 | tf_op jit(solution)/shard_map/conv_general_dilated | solution.py:20
  52.8 1.6 multiply_convert_fusion
  54.4 0.9 fusion.17
  55.3 0.2 convert_reduce_fusion.4
  55.5 0.1 copy-done.6
  55.6 1.5 convert_reduce_fusion.2
  57.1 1.5 convert_reduce_fusion.3
  58.7 4.6 %maximum_convert_fusion.8 = bf16[16,8,8,384]{3,0,2,1:T(8,128)(2,1)S(1)} fusion(bf16[3,3,448,384]{3,2,1,0:T(8,128)(2,1)S(1)} %copy-done, bf16[16,8,8,1152]{3,0,2,1:T(8,128)(2,1)S(1)} %fusion.5), kind=kOutput, calls=%fused_computation.22 | convolution fusion | flops 2665218048 | bytes 4931584 | tf_op jit(solution)/shard_map/conv_general_dilated | solution.py:20
  63.3 1.5 convert_reduce_fusion
  64.7 1.7 convert_reduce_fusion.1
  66.5 0.1 concatenate.7
  66.6 1.1 stack.2
  67.8 6.8 %all-to-all-start = ((f32[8,16,2048]{2,1,0:T(8,128)}), f32[8,16,2048]{2,1,0:T(8,128)}, u32[]{:S(2)}, u32[]{:S(2)}) async-start(f32[8,16,2048]{2,1,0:T(8,128)} %stack.2), calls=%async_computation | async-start | bytes 2097152 | tf_op jit(solution)/shard_map/all_to_all | solution.py:137
  74.6 15.1 %all-to-all-done = f32[8,16,2048]{2,1,0:T(8,128)} async-done(((f32[8,16,2048]{2,1,0:T(8,128)}), f32[8,16,2048]{2,1,0:T(8,128)}, u32[]{:S(2)}, u32[]{:S(2)}) %all-to-all-start) | async-done | bytes 1048608 | tf_op jit(solution)/shard_map/all_to_all | solution.py:137
  89.6 1.3 reduce_sum.69
  90.9 1.3 bitcast_subtract_fusion
  92.3 3.2 fusion.21
  95.5 0.6 dynamic-slice
  96.1 0.8 dynamic-update-slice
  96.8 35.0 %all-reduce = f32[16]{0:T(128)S(1)} all-reduce(f32[16]{0:T(128)S(1)} %dynamic-update-slice), channel_id=1, replica_groups=mesh['sample'=16,'col'=8] {'sample'}, use_global_device_ids=true, to_apply=%add | all-reduce | flops 16 | bytes 128
  131.9 17.6 %all-gather = f32[32768]{0:T(1024)S(1)} all-gather(f32[2048]{0:T(1024)S(1)} %broadcast_multiply_fusion.6), channel_id=2, replica_groups=mesh['sample'=16,'col'=8] {'sample'}, dimensions={0}, use_global_device_ids=true | all-gather | bytes 139264 | tf_op jit(solution)/shard_map/all_gather | solution.py:9
  149.5 143.2 %all-gather.4.cloned.1.call-done = f32[32768,256]{1,0:T(8,128)} async-done(((f32[2048,256]{1,0:T(8,128)}), f32[32768,256]{1,0:T(8,128)}) %all-gather.4.cloned.1.call-update) | async-done | bytes 33554448 | tf_op jit(solution)/shard_map/all_gather | solution.py:9
  292.7 3.0 slice.31
  295.7 102.3 %while.21 = (s32[]{:T(128)}, f32[]{:T(128)}, f32[2048]{0:T(1024)S(1)}, f32[2048,256]{1,0:T(8,128)}, f32[16]{0:T(128)S(1)}, /*index=5*/f32[16,2048]{1,0:T(8,128)S...) while((s32[]{:T(128)}, f32[]{:T(128)}, f32[2048]{0:T(1024)S(1)}, ...), condition=%wide.region_10.11_spmd, body=%wide.region_9.0_spmd.sunk | while | flops 2103305 | bytes 6352095 | solution.py:14
  295.7 0.7 dynamic_slice.82
  298.5 0.1 dynamic_slice.83
  298.6 3.9 fusion.47
  302.5 0.7 dynamic_slice.82
  305.4 0.1 dynamic_slice.83
  305.4 3.9 fusion.47
  309.4 0.7 dynamic_slice.82
  312.2 0.1 dynamic_slice.83
  312.3 3.9 fusion.47
  316.2 0.7 dynamic_slice.82
  319.1 3.9 fusion.47
  323.0 0.7 dynamic_slice.82
  325.9 3.9 fusion.47
  329.8 0.7 dynamic_slice.82
  332.7 3.9 fusion.47
  336.6 0.7 dynamic_slice.82
  339.5 3.9 fusion.47
  343.5 0.7 dynamic_slice.82
  346.4 3.9 fusion.47
  350.3 0.7 dynamic_slice.82
  353.2 3.9 fusion.47
  357.1 0.7 dynamic_slice.82
  360.0 3.9 fusion.47
  363.9 0.7 dynamic_slice.82
  366.8 3.9 fusion.47
  370.7 0.7 dynamic_slice.82
  373.7 3.9 fusion.47
  377.6 0.7 dynamic_slice.82
  380.5 3.9 fusion.47
  384.4 0.7 dynamic_slice.82
  387.3 3.9 fusion.47
  391.2 0.7 dynamic_slice.82
  394.1 3.9 fusion.47
  398.0 1.6 dynamic-slice_multiply_fusion
  (79 shorter events, 1.5 us)
Async XLA Ops:
  7.2 51.5 %copy-start = (bf16[3,3,448,384]{3,2,1,0:T(8,128)(2,1)S(1)}, bf16[3,3,448,384]{3,2,1,0:T(8,128)(2,1)}, u32[]{:S(2)}) copy-start(bf16[3,3,448,384]{3,2,1,0:T(8,128)(2,1)} %param.24) | copy-start | bytes 9289732
  7.2 5.7 %copy-start.2 = (bf16[16,17,17,768]{3,0,2,1:T(8,128)(2,1)S(1)}, bf16[16,17,17,768]{3,0,2,1:T(8,128)(2,1)}, u32[]{:S(2)}) copy-start(bf16[16,17,17,768]{3,0,2,1:T(8,128)(2,1)} %param.15) | copy-start | bytes 21307396
  7.2 5.7 %copy-start.11 = (bf16[1,1,768,384]{3,2,1,0:T(8,128)(2,1)S(1)}, bf16[1,1,768,384]{3,2,1,0:T(8,128)(2,1)}, u32[]{:S(2)}) copy-start(bf16[1,1,768,384]{3,2,1,0:T(8,128)(2,1)} %param.16) | copy-start | bytes 1769476
  12.9 4.1 %copy-start.5 = (bf16[3,3,192,320]{3,2,1,0:T(8,128)(2,1)S(1)}, bf16[3,3,192,320]{3,2,1,0:T(8,128)(2,1)}, u32[]{:S(2)}) copy-start(bf16[3,3,192,320]{3,2,1,0:T(8,128)(2,1)} %param.17) | copy-start | bytes 3317764
  17.0 3.0 copy-start.10
  46.5 6.3 %copy-start.1 = (bf16[16,8,8,1280]{3,0,2,1:T(8,128)(2,1)S(1)}, bf16[16,8,8,1280]{3,0,2,1:T(8,128)(2,1)}, u32[]{:S(2)}) copy-start(bf16[16,8,8,1280]{3,0,2,1:T(8,128)(2,1)} %concatenate.6) | copy-start | bytes 7864324
  46.5 6.3 %copy-start.4 = (f32[8,8]{1,0:T(8,128)S(1)}, f32[8,8]{1,0:T(8,128)}, u32[]{:S(2)}) copy-start(f32[8,8]{1,0:T(8,128)} %constant.112.clone.1) | copy-start | bytes 772
  52.8 1.6 copy-start.12
  54.4 1.2 copy-start.6
  55.6 1.5 copy-start.7
  58.6 4.6 %copy-start.8 = (bf16[3,1,384,384]{3,2,1,0:T(8,128)(2,1)S(1)}, bf16[3,1,384,384]{3,2,1,0:T(8,128)(2,1)}, u32[]{:S(2)}) copy-start(bf16[3,1,384,384]{3,2,1,0:T(8,128)(2,1)} %param.26) | copy-start | bytes 2654212
  63.2 1.5 copy-start.9
  67.8 21.9 %all-to-all-start = ((f32[8,16,2048]{2,1,0:T(8,128)}), f32[8,16,2048]{2,1,0:T(8,128)}, u32[]{:S(2)}, u32[]{:S(2)}) async-start(f32[8,16,2048]{2,1,0:T(8,128)} %stack.2), calls=%async_computation | async-start | bytes 2097152 | tf_op jit(solution)/shard_map/all_to_all | solution.py:137
  74.6 218.1 %all-gather.4.cloned.1.call-start = ((), (), s32[]{:S(2)}) async-start(), calls=%async_computation.1 | async-start | bytes 35651584 | tf_op jit(solution)/shard_map/all_gather | solution.py:9
  92.3 3.2 copy-start.13
  398.0 1.6 copy-start.3
Sparse Core Ops, SparseCore 0:
  95.6 197.0 all-gather.3
